TPU v7x, 32 devices: a whole 2x2x4 slice. The times are simulated.
32 devices in a mesh: grp: 16 (over z, x, core), uly: 2 (over y).
Axes of the slice: x: 2, y: 2, z: 4, core: 2. Of those that a mesh axis runs over, the one named last changes fastest.
Arguments:
- queries: bfloat16 [4096, 32, 128], P(('grp', 'uly')), may hold values from -16 to 16
- keys: bfloat16 [4096, 4, 128], P(('grp', 'uly')), may hold values from -8 to 8
- values: bfloat16 [4096, 4, 128], P(('grp', 'uly')), may hold values from -6 to 6
- output_cotangent: bfloat16 [4096, 32, 128], P(('grp', 'uly')), may hold values from -6 to 6
- block_lists: int32 [128, 1], replicated, may hold values from 0 to 127, as said below
- list_counts: int32 [128], replicated, may hold values from 0 to 1, as said below
Outputs:
- attended: bfloat16 [4096, 32, 128], P(('grp', 'uly'))
- query_grad: bfloat16 [4096, 32, 128], P(('grp', 'uly'))
- key_gradient: bfloat16 [4096, 4, 128], P(('grp', 'uly'))
- value_gradient: bfloat16 [4096, 4, 128], P(('grp', 'uly'))
Inputs may be any that keep to these rules, and one draw needn't show every extreme that they name: `block_lists`: calling an aligned run of 8 blocks a group: every entry of block b's list is a block of another group than b's, and the entries of all lists of one group, counted or not, lie in pairwise different groups. `list_counts`: some block counts all 1 entries in every draw.
All inputs are finite; a program needn't handle non-finite values.
Results may differ from a plain program's by a relative error of at most 0.039.
Values may be sent and summed in bfloat16 or wider, within the bound.
No kernel may reach another device: no remote copies, remote signals or barrier semaphores. Data moves between devices by JAX's collectives and lax.ppermute only.
A program may use at most 128 MiB of HBM per device.

v0:
```python
import jax
import jax.numpy as jnp
from jax import lax
from jax.sharding import PartitionSpec as P


def on_device(queries, keys, values, output_cotangent, block_lists, list_counts):
    uly_count = lax.axis_size("uly")
    grp_count = lax.axis_size("grp")
    my_group = lax.axis_index("grp")
    tokens, head_count, head_width = queries.shape
    kv_heads = keys.shape[1]
    copies = max(1, uly_count // kv_heads)
    blocks_all, remote = block_lists.shape
    per_group = blocks_all // grp_count
    block_tok = tokens * uly_count // per_group
    group_tok = tokens * uly_count
    score_scale = head_width ** (-0.5)
    lists = block_lists.reshape(grp_count, per_group, remote)
    counted = (jnp.arange(remote)[None, :] < list_counts[:, None]).reshape(
        grp_count, per_group, remote
    )
    wanted = (lists // per_group == my_group) & counted
    send_place = jnp.sum(jnp.where(wanted, lists % per_group, 0), axis=(1, 2))
    sending = jnp.any(wanted, axis=(1, 2))
    mine_source = lax.dynamic_index_in_dim(lists, my_group, 0, keepdims=False) // per_group
    mine_counted = lax.dynamic_index_in_dim(counted, my_group, 0, keepdims=False)
    trip_count = jnp.max(jnp.sum(mine_counted.astype(jnp.int32), axis=1))

    def to_blocks(array_in):
        return array_in.reshape((per_group, block_tok) + array_in.shape[1:])

    keys_wide = jnp.repeat(keys, copies, axis=1)
    values_wide = jnp.repeat(values, copies, axis=1)
    query_heads, grad_heads, key_heads, value_heads = (
        lax.all_to_all(queries, "uly", split_axis=1, concat_axis=0, tiled=True),
        lax.all_to_all(output_cotangent, "uly", split_axis=1, concat_axis=0, tiled=True),
        lax.all_to_all(keys_wide, "uly", split_axis=1, concat_axis=0, tiled=True),
        lax.all_to_all(values_wide, "uly", split_axis=1, concat_axis=0, tiled=True),
    )
    stacked = jnp.stack([to_blocks(key_heads), to_blocks(value_heads)])
    outgoing = jnp.take(stacked, send_place, axis=1)
    arrived = lax.all_to_all(outgoing, "grp", split_axis=1, concat_axis=1, tiled=True)
    kv_local = key_heads.shape[1]
    heads_local = query_heads.shape[1]
    heads_per_group = heads_local // kv_local
    query_blk = query_heads.reshape(per_group, block_tok, kv_local, heads_per_group, head_width)
    grad_blk = grad_heads.reshape(per_group, block_tok, kv_local, heads_per_group, head_width)
    key_blk = to_blocks(key_heads)
    value_blk = to_blocks(value_heads)
    far_keys = arrived[0]
    far_values = arrived[1]
    causal = jnp.arange(block_tok)[:, None] >= jnp.arange(block_tok)[None, :]

    def logits(key_rows):
        return (
            jnp.einsum("pqkgd,pjkd->pkgqj", query_blk, key_rows, preferred_element_type=jnp.float32)
            * score_scale
        )

    def slot_rows(slot_index):
        source = lax.dynamic_index_in_dim(mine_source, slot_index, 1, keepdims=False)
        counted_slot = lax.dynamic_index_in_dim(mine_counted, slot_index, 1, keepdims=False)
        return (
            jnp.take(far_keys, source, axis=0),
            jnp.take(far_values, source, axis=0),
            counted_slot,
            source,
        )

    def masked(scores, counted_slot):
        return jnp.where(counted_slot[:, None, None, None, None], scores, -jnp.inf)

    near_scores = jnp.where(causal, logits(key_blk), -jnp.inf)
    highest = jnp.max(near_scores, axis=-1)
    denominator = jnp.sum(jnp.exp(near_scores - highest[..., None]), axis=-1)

    def max_sweep(slot_index, state_pair):
        highest, denominator = state_pair
        key_rows, value_rows, counted_slot, source = slot_rows(slot_index)
        scores = masked(logits(key_rows), counted_slot)
        new_highest = jnp.maximum(highest, jnp.max(scores, axis=-1))
        denominator = denominator * jnp.exp(highest - new_highest) + jnp.sum(
            jnp.exp(scores - new_highest[..., None]), axis=-1
        )
        return (new_highest, denominator)

    highest, denominator = lax.fori_loop(0, trip_count, max_sweep, (highest, denominator))
    log_total = highest + jnp.log(denominator)

    def softmax_weights(scores):
        return jnp.exp(scores - log_total[..., None])

    summed = jnp.einsum(
        "pkgqj,pjkd->pqkgd",
        softmax_weights(near_scores).astype(jnp.bfloat16),
        value_blk,
        preferred_element_type=jnp.float32,
    )

    def value_sweep(slot_index, summed):
        key_rows, value_rows, counted_slot, source = slot_rows(slot_index)
        weights = softmax_weights(masked(logits(key_rows), counted_slot)).astype(jnp.bfloat16)
        return summed + jnp.einsum(
            "pkgqj,pjkd->pqkgd", weights, value_rows, preferred_element_type=jnp.float32
        )

    summed = lax.fori_loop(0, trip_count, value_sweep, summed)
    attended_blk = summed.astype(jnp.bfloat16)
    row_delta = jnp.transpose(
        jnp.sum(grad_blk.astype(jnp.float32) * attended_blk.astype(jnp.float32), axis=-1),
        (0, 2, 3, 1),
    )

    def backward(scores, key_rows, value_rows):
        probs = softmax_weights(scores)
        weights = probs.astype(jnp.bfloat16)
        dprobs = jnp.einsum(
            "pqkgd,pjkd->pkgqj", grad_blk, value_rows, preferred_element_type=jnp.float32
        )
        dscores = (probs * (dprobs - row_delta[..., None])).astype(jnp.bfloat16)
        query_term = jnp.einsum(
            "pkgqj,pjkd->pqkgd", dscores, key_rows, preferred_element_type=jnp.float32
        )
        key_term = (
            jnp.einsum("pkgqj,pqkgd->pjkd", dscores, query_blk, preferred_element_type=jnp.float32)
            * score_scale
        )
        value_term = jnp.einsum(
            "pkgqj,pqkgd->pjkd", weights, grad_blk, preferred_element_type=jnp.float32
        )
        return (query_term, key_term, value_term)

    query_sum, key_near, value_near = backward(near_scores, key_blk, value_blk)
    far_grads = jnp.zeros((2, grp_count, block_tok, kv_local, head_width), jnp.float32)

    def grad_sweep(slot_index, state_pair):
        query_sum, far_grads = state_pair
        key_rows, value_rows, counted_slot, source = slot_rows(slot_index)
        query_term, key_term, value_term = backward(
            masked(logits(key_rows), counted_slot), key_rows, value_rows
        )
        routing = (
            (source[:, None] == jnp.arange(grp_count)[None, :]) & counted_slot[:, None]
        ).astype(jnp.float32)
        routed = jnp.einsum(
            "ps,xpjkd->xsjkd",
            routing,
            jnp.stack([key_term, value_term]),
            precision=lax.Precision.HIGHEST,
        )
        return (query_sum + query_term, far_grads + routed)

    query_sum, far_grads = lax.fori_loop(0, trip_count, grad_sweep, (query_sum, far_grads))
    owners = ((send_place[:, None] == jnp.arange(per_group)[None, :]) & sending[:, None]).astype(
        jnp.float32
    )
    returned = lax.all_to_all(far_grads, "grp", split_axis=1, concat_axis=1, tiled=True)
    landed = jnp.einsum("sp,xsjkd->xpjkd", owners, returned, precision=lax.Precision.HIGHEST)
    key_local = (key_near + landed[0]).reshape(group_tok, kv_local, head_width)
    value_local = (value_near + landed[1]).reshape(group_tok, kv_local, head_width)
    attended_rows = attended_blk.reshape(group_tok, heads_local, head_width)
    query_rows = (
        (query_sum * score_scale).astype(jnp.bfloat16).reshape(group_tok, heads_local, head_width)
    )
    attended, query_grad = (
        lax.all_to_all(attended_rows, "uly", split_axis=0, concat_axis=1, tiled=True),
        lax.all_to_all(query_rows, "uly", split_axis=0, concat_axis=1, tiled=True),
    )
    key_parts, value_parts = (
        lax.all_to_all(key_local, "uly", split_axis=0, concat_axis=1, tiled=True),
        lax.all_to_all(value_local, "uly", split_axis=0, concat_axis=1, tiled=True),
    )
    key_gradient = jnp.sum(key_parts.reshape(tokens, kv_heads, copies, head_width), axis=2).astype(
        jnp.bfloat16
    )
    value_gradient = jnp.sum(
        value_parts.reshape(tokens, kv_heads, copies, head_width), axis=2
    ).astype(jnp.bfloat16)
    return (attended, query_grad, key_gradient, value_gradient)


def solution(mesh):
    placed = (
        P(("grp", "uly"), None, None),
        P(("grp", "uly"), None, None),
        P(("grp", "uly"), None, None),
        P(("grp", "uly"), None, None),
        P(),
        P(),
    )
    return jax.shard_map(
        on_device,
        mesh=mesh,
        in_specs=placed,
        out_specs=(
            P(("grp", "uly"), None, None),
            P(("grp", "uly"), None, None),
            P(("grp", "uly"), None, None),
            P(("grp", "uly"), None, None),
        ),
        check_vma=False,
    )
```

profile of v0, /device:TPU:0, one launch (start us, length us, event | category | flops | bytes accessed | tf_op | source)
XLA Modules:
  0.0 215.2 jit_solution(12773727700696270377)
XLA Ops:
  0.6 1.7 copy.88
  2.3 4.2 %all-to-all-start = ((bf16[128,4,128]{2,0,1:T(8,128)(2,1)}), bf16[128,4,128]{2,0,1:T(8,128)(2,1)S(1)}, u32[]{:S(2)}, u32[]{:S(2)}) async-start(bf16[128,4,128]{2,0,1:T(8,128)(2,1)} %copy.88), calls=%async_computation | async-start | bytes 262144 | tf_op jit(solution)/shard_map/all_to_all | solution.py:38
  7.1 1.3 reduce.3
  8.5 0.7 broadcast_compare_fusion
  9.2 0.6 fusion.93
  9.9 1.6 copy.96
  11.4 2.6 %copy.90 = bf16[128,32,128]{2,0,1:T(8,128)(2,1)} copy(bf16[128,32,128]{2,1,0:T(8,128)(2,1)} %param.14) | data formatting | bytes 2097152 | tf_op args[0]
  14.0 1.4 copy.108
  15.4 3.4 %all-to-all-start.2 = ((bf16[128,4,128]{2,0,1:T(8,128)(2,1)}), bf16[128,4,128]{2,0,1:T(8,128)(2,1)S(1)}, u32[]{:S(2)}, u32[]{:S(2)}) async-start(bf16[128,4,128]{2,0,1:T(8,128)(2,1)} %copy.96), calls=%async_computation.2 | async-start | bytes 262144 | tf_op jit(solution)/shard_map/all_to_all | solution.py:39
  18.9 4.4 %all-to-all-done.2 = bf16[128,4,128]{2,0,1:T(8,128)(2,1)S(1)} async-done(((bf16[128,4,128]{2,0,1:T(8,128)(2,1)}), bf16[128,4,128]{2,0,1:T(8,128)(2,1)S(1)}, u32[]{:S(2)}, u32[]{:S(2)}) %all-to-all-start.2) | async-done | bytes 131104 | tf_op jit(solution)/shard_map/all_to_all | solution.py:39
  23.4 3.6 %all-to-all-start.1 = ((bf16[128,32,128]{2,0,1:T(8,128)(2,1)}), bf16[128,32,128]{2,0,1:T(8,128)(2,1)S(1)}, u32[]{:S(2)}, u32[]{:S(2)}) async-start(bf16[128,32,128]{2,0,1:T(8,128)(2,1)} %copy.90), calls=%async_computation.1 | async-start | bytes 2097152 | tf_op jit(solution)/shard_map/all_to_all | solution.py:36
  27.0 12.9 %all-to-all-done.1 = bf16[128,32,128]{2,0,1:T(8,128)(2,1)S(1)} async-done(((bf16[128,32,128]{2,0,1:T(8,128)(2,1)}), bf16[128,32,128]{2,0,1:T(8,128)(2,1)S(1)}, u32[]{:S(2)}, u32[]{:S(2)}) %all-to-all-start.1) | async-done | bytes 1048608 | tf_op jit(solution)/shard_map/all_to_all | solution.py:36
  39.9 3.6 %all-to-all-start.5 = ((bf16[128,32,128]{2,0,1:T(8,128)(2,1)}), bf16[128,32,128]{2,0,1:T(8,128)(2,1)S(1)}, u32[]{:S(2)}, u32[]{:S(2)}) async-start(bf16[128,32,128]{2,0,1:T(8,128)(2,1)} %copy.108), calls=%async_computation.5 | async-start | bytes 2097152 | tf_op jit(solution)/shard_map/all_to_all | solution.py:37
  43.5 0.7 convert_reduce_fusion
  44.3 0.6 gather_fusion
  45.0 0.9 select_bitcast_fusion
  45.9 9.7 %all-to-all-done.5 = bf16[128,32,128]{2,0,1:T(8,128)(2,1)S(1)} async-done(((bf16[128,32,128]{2,0,1:T(8,128)(2,1)}), bf16[128,32,128]{2,0,1:T(8,128)(2,1)S(1)}, u32[]{:S(2)}, u32[]{:S(2)}) %all-to-all-start.5) | async-done | bytes 1048608 | tf_op jit(solution)/shard_map/all_to_all | solution.py:37
  55.6 5.9 %all-to-all-start.3 = ((bf16[2,16,32,2,128]{4,2,3,0,1:T(8,128)(2,1)}), bf16[2,16,32,2,128]{4,2,3,0,1:T(8,128)(2,1)}, u32[]{:S(2)}, u32[]{:S(2)}) async-start(bf16[2,16,32,2,128]{4,2,3,0,1:T(8,128)(2,1)} %select_bitcast_fusion), calls=%async_computation.3 | async-start | bytes 1048576 | tf_op jit(solution)/shard_map/all_to_all | solution.py:43
  61.6 0.7 copy.92
  62.3 2.3 %copy.110 = bf16[2,128,16,128]{3,2,1,0:T(8,128)(2,1)S(1)} copy(bf16[2,128,16,128]{3,1,2,0:T(8,128)(2,1)} %bitcast.255) | data formatting | bytes 2097152 | tf_op jit(solution)/shard_map/all_to_all | solution.py:37
  64.6 1.8 fusion.96
  66.4 1.3 copy-done.2
  67.7 1.3 exponential_reduce_fusion
  69.0 7.0 %all-to-all-done.3 = bf16[2,16,32,2,128]{4,2,3,0,1:T(8,128)(2,1)} async-done(((bf16[2,16,32,2,128]{4,2,3,0,1:T(8,128)(2,1)}), bf16[2,16,32,2,128]{4,2,3,0,1:T(8,128)(2,1)}, u32[]{:S(2)}, u32[]{:S(2)}) %all-to-all-start.3) | async-done | bytes 524320 | tf_op jit(solution)/shard_map/all_to_all | solution.py:43
  76.0 1.1 slice_bitcast_fusion.2
  78.4 1.8 fusion.57
  80.2 1.3 copy-done.8
  81.5 3.0 %copy.101 = f32[8,2,32,32,8]{3,4,2,1,0:T(8,128)} copy(f32[8,2,32,32,8]{3,2,4,1,0:T(8,128)S(1)} %fusion.57) | data formatting | bytes 1048576 | tf_op jit(solution)/shard_map/while | solution.py:88
  84.5 1.9 copy.105
  86.4 4.7 %while.43 = (s32[]{:T(128)}, f32[8,2,8,32]{3,2,1,0:T(8,128)S(1)}, f32[8,2,8,32]{3,2,1,0:T(8,128)}, s32[]{:T(128)}, pred[8,1]{0,1:T(4,128)(4,1)S(1)}, /*index=5*/f32[8,2,32,32,8]{3,4,2,1,0:T(8,128)}, s32[]{:T(128)}) while((s32[]{:T(128)}, f32[8,2,8,32]{3,2,1,0:T(8,128)S(1)}, f32[8,2,8,32]{3,2,1,0:T(8,128)}, s32[]{:T(128)}, ...), condition=%wide.region_7.9_spmd, body=%wide.region_4.8_spmd.sunk | while | flops 925698 | bytes 3489969 | solution.py:88
  87.0 2.1 bitcast_reduce_fusion.2
  91.1 0.9 log_add_fusion
  92.0 3.5 %convolution_bitcast_fusion.1 = f32[8,32,2,8,128]{4,1,3,2,0:T(8,128)} fusion(f32[8,2,8,32,32]{3,4,2,1,0:T(8,128)} %copy-done.2, f32[8,2,8,32]{3,2,1,0:T(8,128)S(1)} %log_add_fusion, bf16[8,32,2,128,1]{3,1,0,2,4:T(8,128)(2,1)} %bitcast.260), kind=kOutput, calls=%fused_computation.52 | convolution fusion | flops 33816576 | bytes 2768896 | tf_op jit(solution)/shard_map/pkgqj,pjkd->pqkgd/dot_general | solution.py:94
  95.5 4.7 %while.44 = (s32[]{:T(128)}, f32[8,32,2,8,128]{4,1,3,2,0:T(8,128)}, s32[]{:T(128)}, pred[8,1]{0,1:T(4,128)(4,1)S(1)}, f32[8,2,32,32,8]{2,3,4,1,0:T(8,128)S(1)}, ...) while((s32[]{:T(128)}, f32[8,32,2,8,128]{4,1,3,2,0:T(8,128)}, s32[]{:T(128)}, ...), condition=%wide.region_9.11_spmd, body=%wide.region_8.10_spmd.sunk | while | flops 34603008 | bytes 4866141 | solution.py:108
  96.1 3.3 %bitcast_add_fusion.6 = f32[8,32,2,8,128]{4,1,3,2,0:T(8,128)} fusion(f32[8,32,2,8,128]{4,1,3,2,0:T(8,128)} %get-tuple-element.814, f32[8,2,32,32,8]{2,3,4,1,0:T(8,128)S(1)} %get-tuple-element.825, f32[8,2,8,32]{3,2,1,0:T(8,128)S(1)} %get-tuple-element.826, pred[8]{0:T(512)(128)(4,1)S(1)} %bitcast.277, bf16[8,32,2,128]{3,1,2,0:T(8,128)(2,1)S(1)} %get-tuple-element.827), kind=kOutput, calls=%fused_computation.9.clone.1 | convolution fusion | flops 34603008 | bytes 4866056 | tf_op jit(solution)/shard_map/while/body/pkgqj,pjkd->pqkgd/dot_general | solution.py:104
  100.2 3.1 %fusion.52 = f32[8,2,32,32,8]{3,2,4,1,0:T(8,128)} fusion(bf16[8,32,2,8,128]{4,3,2,1,0:T(8,128)(2,1)S(1)} %bitcast.243, bf16[8,32,2,128]{3,1,2,0:T(8,128)(2,1)S(1)} %get-tuple-element.868), kind=kOutput, calls=%fused_computation.76 | convolution fusion | flops 33554432 | bytes 1703936 | tf_op jit(solution)/shard_map/while/body/pqkgd,pjkd->pkgqj/dot_general | solution.py:118
  103.4 3.2 %multiply_reduce_fusion = (f32[8,32,2,8]{3,2,1,0:T(2,128)}, bf16[8,32,2,8,128]{4,3,2,1,0:T(8,128)(2,1)}) fusion(bf16[8,32,2,8,128]{4,3,2,1,0:T(8,128)(2,1)S(1)} %bitcast.244, f32[8,32,2,8,128]{4,1,3,2,0:T(8,128)S(1)} %copy-done.1), kind=kLoop, calls=%fused_computation.47 | loop fusion | flops 2093056 | bytes 4210688 | tf_op jit(solution)/shard_map/reduce_sum | solution.py:111
  106.6 1.0 copy.113
  107.6 3.3 %convolution_bitcast_fusion.4 = f32[1,8,32,2,128]{4,2,3,1,0:T(8,128)} fusion(f32[8,2,32,32,8]{3,2,4,1,0:T(8,128)} %copy-done.8, f32[8,2,8,32]{3,2,1,0:T(8,128)S(1)} %get-tuple-element.866, pred[8]{0:T(512)(128)(4,1)S(1)} %get-tuple-element.627, bf16[8,32,2,8,128]{4,3,2,1,0:T(8,128)(2,1)S(1)} %bitcast.245), kind=kOutput, calls=%fused_computation.56 | convolution fusion | flops 34078720 | bytes 1851400 | tf_op jit(solution)/shard_map/while/body/pkgqj,pqkgd->pjkd/dot_general | solution.py:129
  110.9 2.8 %fusion.28 = bf16[8,2,8,32,32]{3,4,2,1,0:T(8,128)(2,1)} fusion(f32[8,2,8,32,32]{3,4,2,1,0:T(8,128)S(1)} %copy-done.3, f32[8,2,8,32]{3,2,1,0:T(8,128)S(1)} %copy.113, f32[8,2,8,32]{3,2,1,0:T(8,128)S(1)} %get-tuple-element.866, bf16[8,32,2,8,128]{4,3,2,1,0:T(8,128)(2,1)S(1)} %bitcast.246, bf16[8,32,2,128,1]{3,1,0,2,4:T(8,128)(2,1)S(1)} %bitcast.261), kind=kOutput, calls=%fused_computation.42 | convolution fusion | flops 34078720 | bytes 1998848 | tf_op jit(solution)/shard_map/pqkgd,pjkd->pkgqj/dot_general | solution.py:118
  113.7 1.0 fusion.33
  114.7 2.9 %copy.121 = f32[8,2,32,32,8]{2,3,4,1,0:T(8,128)} copy(f32[8,2,32,32,8]{3,2,4,1,0:T(8,128)} %fusion.52) | data formatting | bytes 1048576 | tf_op jit(solution)/shard_map/while | solution.py:154
  117.7 0.9 fusion.60
  118.6 1.5 copy.123
  120.1 1.8 convolution_bitcast_fusion
  122.4 6.0 %while.45 = (s32[]{:T(128)}, f32[8,32,2,8,128]{4,1,3,2,0:T(8,128)}, f32[2,16,32,2,128]{4,3,2,1,0:T(2,128)S(1)}, s32[]{:T(128)}, pred[8,1]{0,1:T(4,128)(4,1)S(1)}...) while((s32[]{:T(128)}, f32[8,32,2,8,128]{4,1,3,2,0:T(8,128)}, ...), condition=%wide.region_12.14_spmd, body=%wide.region_11.13_spmd.sunk | while | flops 35127296 | bytes 12746905 | solution.py:154
  123.1 4.1 %bitcast_add_fusion.7 = f32[8,32,2,8,128]{4,1,3,2,0:T(8,128)} fusion(f32[8,32,2,8,128]{4,1,3,2,0:T(8,128)} %get-tuple-element.842, f32[8,2,32,32,8]{2,3,4,1,0:T(8,128)} %get-tuple-element.860, f32[8,2,32,32,8]{2,3,4,1,0:T(8,128)S(1)} %get-tuple-element.858, f32[8,2,8,32]{3,2,1,0:T(8,128)S(1)} %get-tuple-element.861, ...), kind=kOutput, calls=%fused_computation.20.clone.1 | convolution fusion | flops 34865152 | bytes 5406728 | tf_op jit(solution)/shard_map/while/body/pkgqj,pjkd->pqkgd/dot_general | solution.py:122
  128.4 4.0 %fusion.29 = bf16[8,32,2,8,128]{4,3,2,1,0:T(8,128)(2,1)} fusion(f32[8,32,2,8,128]{4,1,3,2,0:T(8,128)} %get-tuple-element.466), kind=kLoop, calls=%fused_computation.45 | loop fusion | flops 1048576 | bytes 3145728 | tf_op jit(solution)/shard_map/convert_element_type | solution.py:164
  132.4 3.6 %all-to-all-start.6 = ((bf16[256,16,128]{2,1,0:T(8,128)(2,1)}), bf16[256,16,128]{2,1,0:T(8,128)(2,1)S(1)}, u32[]{:S(2)}, u32[]{:S(2)}) async-start(bf16[256,16,128]{2,1,0:T(8,128)(2,1)} %bitcast.69), calls=%async_computation.6 | async-start | bytes 2097152 | tf_op jit(solution)/shard_map/all_to_all | solution.py:168
  136.1 13.9 %all-to-all-done.6 = bf16[256,16,128]{2,1,0:T(8,128)(2,1)S(1)} async-done(((bf16[256,16,128]{2,1,0:T(8,128)(2,1)}), bf16[256,16,128]{2,1,0:T(8,128)(2,1)S(1)}, u32[]{:S(2)}, u32[]{:S(2)}) %all-to-all-start.6) | async-done | bytes 1048608 | tf_op jit(solution)/shard_map/all_to_all | solution.py:168
  150.0 29.1 %all_to_all.124 = f32[2,16,32,2,128]{4,3,2,0,1:T(2,128)} all-to-all(f32[2,16,32,2,128]{4,3,2,0,1:T(2,128)S(1)} %copy.127), channel_id=1, replica_groups=mesh['grp'=16,'uly'=2] {'grp'}, dimensions={1} | all-to-all | bytes 2097152 | tf_op jit(solution)/shard_map/all_to_all | solution.py:158
  179.1 4.9 %all-to-all-start.4 = ((bf16[256,16,128]{2,1,0:T(8,128)(2,1)}), bf16[256,16,128]{2,1,0:T(8,128)(2,1)}, u32[]{:S(2)}, u32[]{:S(2)}) async-start(bf16[256,16,128]{2,1,0:T(8,128)(2,1)} %bitcast.252), calls=%async_computation.4 | async-start | bytes 2097152 | tf_op jit(solution)/shard_map/all_to_all | solution.py:167
  184.1 2.2 %fusion.39 = f32[2,32,2,128,8]{3,4,2,1,0:T(8,128)S(1)} fusion(f32[2,16,32,2,128]{4,3,2,0,1:T(2,128)} %all_to_all.124, s32[16]{0:T(128)S(1)} %copy-done.28, pred[16]{0:T(512)(128)(4,1)S(1)} %copy-done.26), kind=kOutput, calls=%fused_computation.64 | convolution fusion | flops 25166080 | bytes 1572944 | tf_op jit(solution)/shard_map/sp,xsjkd->xpjkd/dot_general | solution.py:159
  187.3 0.8 copy.136
  188.1 10.6 %all-to-all-done.4 = bf16[256,16,128]{2,1,0:T(8,128)(2,1)} async-done(((bf16[256,16,128]{2,1,0:T(8,128)(2,1)}), bf16[256,16,128]{2,1,0:T(8,128)(2,1)}, u32[]{:S(2)}, u32[]{:S(2)}) %all-to-all-start.4) | async-done | bytes 1048608 | tf_op jit(solution)/shard_map/all_to_all | solution.py:167
  198.7 3.4 %all-to-all-start.9 = ((bf16[256,2,128]{2,1,0:T(2,128)(2,1)}), bf16[256,2,128]{2,1,0:T(2,128)(2,1)S(1)}, u32[]{:S(2)}, u32[]{:S(2)}) async-start(bf16[256,2,128]{2,1,0:T(2,128)(2,1)} %copy.136), calls=%async_computation.9 | async-start | bytes 262144 | tf_op jit(solution)/shard_map/all_to_all | solution.py:172
  202.1 2.1 fusion.36
  204.2 0.8 copy.131
  205.0 1.6 all-to-all-done.9
  206.6 3.4 %all-to-all-start.8 = ((bf16[256,2,128]{2,1,0:T(2,128)(2,1)}), bf16[256,2,128]{2,1,0:T(2,128)(2,1)S(1)}, u32[]{:S(2)}, u32[]{:S(2)}) async-start(bf16[256,2,128]{2,1,0:T(2,128)(2,1)} %copy.131), calls=%async_computation.8 | async-start | bytes 262144 | tf_op jit(solution)/shard_map/all_to_all | solution.py:171
  210.0 1.2 copy.125
  211.1 2.4 %copy.107 = bf16[128,2,16,128]{3,2,1,0:T(8,128)(2,1)} copy(bf16[128,2,16,128]{3,2,0,1:T(8,128)(2,1)} %bitcast.44) | data formatting | bytes 2097152 | tf_op jit(solution)/shard_map/all_to_all | solution.py:167
  213.5 0.8 copy.140
  214.5 0.8 copy.139
  (93 shorter events, 6.0 us)
Async XLA Ops:
  0.6 13.4 %copy-start.24 = (bf16[128,32,128]{2,1,0:T(8,128)(2,1)S(1)}, bf16[128,32,128]{2,1,0:T(8,128)(2,1)}, u32[]{:S(2)}) copy-start(bf16[128,32,128]{2,1,0:T(8,128)(2,1)} %param.17) | copy-start | bytes 3145732
  2.3 13.1 %all-to-all-start = ((bf16[128,4,128]{2,0,1:T(8,128)(2,1)}), bf16[128,4,128]{2,0,1:T(8,128)(2,1)S(1)}, u32[]{:S(2)}, u32[]{:S(2)}) async-start(bf16[128,4,128]{2,0,1:T(8,128)(2,1)} %copy.88), calls=%async_computation | async-start | bytes 262144 | tf_op jit(solution)/shard_map/all_to_all | solution.py:38
  15.4 7.9 %all-to-all-start.2 = ((bf16[128,4,128]{2,0,1:T(8,128)(2,1)}), bf16[128,4,128]{2,0,1:T(8,128)(2,1)S(1)}, u32[]{:S(2)}, u32[]{:S(2)}) async-start(bf16[128,4,128]{2,0,1:T(8,128)(2,1)} %copy.96), calls=%async_computation.2 | async-start | bytes 262144 | tf_op jit(solution)/shard_map/all_to_all | solution.py:39
  18.9 21.0 %copy-start.27 = (s32[16]{0:T(128)}, s32[16]{0:T(128)S(1)}, u32[]{:S(2)}) copy-start(s32[16]{0:T(128)S(1)} %fusion.72) | copy-start | bytes 196
  23.4 16.6 %all-to-all-start.1 = ((bf16[128,32,128]{2,0,1:T(8,128)(2,1)}), bf16[128,32,128]{2,0,1:T(8,128)(2,1)S(1)}, u32[]{:S(2)}, u32[]{:S(2)}) async-start(bf16[128,32,128]{2,0,1:T(8,128)(2,1)} %copy.90), calls=%async_computation.1 | async-start | bytes 2097152 | tf_op jit(solution)/shard_map/all_to_all | solution.py:36
  39.9 15.7 %all-to-all-start.5 = ((bf16[128,32,128]{2,0,1:T(8,128)(2,1)}), bf16[128,32,128]{2,0,1:T(8,128)(2,1)S(1)}, u32[]{:S(2)}, u32[]{:S(2)}) async-start(bf16[128,32,128]{2,0,1:T(8,128)(2,1)} %copy.108), calls=%async_computation.5 | async-start | bytes 2097152 | tf_op jit(solution)/shard_map/all_to_all | solution.py:37
  44.2 20.4 %copy-start.19 = (bf16[2,128,2,128]{3,1,0,2:T(8,128)(2,1)}, bf16[2,128,2,128]{3,1,0,2:T(8,128)(2,1)S(1)}, u32[]{:S(2)}) copy-start(bf16[2,128,2,128]{3,1,0,2:T(8,128)(2,1)S(1)} %copy.89) | copy-start | bytes 393220
  44.2 11.4 %copy-start.21 = (bf16[2,128,2,128]{3,1,0,2:T(8,128)(2,1)}, bf16[2,128,2,128]{3,1,0,2:T(8,128)(2,1)S(1)}, u32[]{:S(2)}) copy-start(bf16[2,128,2,128]{3,1,0,2:T(8,128)(2,1)S(1)} %copy.97) | copy-start | bytes 393220
  55.6 6.7 %copy-start.16 = (bf16[128,32,128]{2,0,1:T(8,128)(2,1)}, bf16[128,32,128]{2,0,1:T(8,128)(2,1)S(1)}, u32[]{:S(2)}) copy-start(bf16[128,32,128]{2,0,1:T(8,128)(2,1)S(1)} %all-to-all-done.5) | copy-start | bytes 3145732
  55.6 20.4 %all-to-all-start.3 = ((bf16[2,16,32,2,128]{4,2,3,0,1:T(8,128)(2,1)}), bf16[2,16,32,2,128]{4,2,3,0,1:T(8,128)(2,1)}, u32[]{:S(2)}, u32[]{:S(2)}) async-start(bf16[2,16,32,2,128]{4,2,3,0,1:T(8,128)(2,1)} %select_bitcast_fusion), calls=%async_computation.3 | async-start | bytes 1048576 | tf_op jit(solution)/shard_map/all_to_all | solution.py:43
  62.3 16.1 %copy-start.10 = (bf16[2,128,16,128]{3,2,1,0:T(8,128)(2,1)}, bf16[2,128,16,128]{3,2,1,0:T(8,128)(2,1)S(1)}, u32[]{:S(2)}) copy-start(bf16[2,128,16,128]{3,2,1,0:T(8,128)(2,1)S(1)} %copy.92) | copy-start | bytes 3145732
  64.6 46.3 %copy-start.6 = (bf16[2,128,16,128]{3,2,1,0:T(8,128)(2,1)}, bf16[2,128,16,128]{3,2,1,0:T(8,128)(2,1)S(1)}, u32[]{:S(2)}) copy-start(bf16[2,128,16,128]{3,2,1,0:T(8,128)(2,1)S(1)} %copy.110) | copy-start | bytes 3145732
  66.4 1.4 copy-start.2
  80.1 1.3 copy-start.8
  87.0 2.2 %copy-start = (f32[8,2,32,32,8]{3,4,2,1,0:T(8,128)S(1)}, f32[8,2,32,32,8]{3,4,2,1,0:T(8,128)}, u32[]{:S(2)}) copy-start(f32[8,2,32,32,8]{3,4,2,1,0:T(8,128)} %get-tuple-element.803) | copy-start | bytes 1572868 | tf_op jit(solution)/shard_map/while
  87.0 2.8 %copy-start.17 = (f32[8,2,8,32]{3,2,1,0:T(8,128)S(1)}, f32[8,2,8,32]{3,2,1,0:T(8,128)}, u32[]{:S(2)}) copy-start(f32[8,2,8,32]{3,2,1,0:T(8,128)} %get-tuple-element.793) | copy-start | bytes 49156 | tf_op jit(solution)/shard_map/while
  89.8 0.6 copy-start.18
  100.2 3.1 %copy-start.1 = (f32[8,32,2,8,128]{4,1,3,2,0:T(8,128)S(1)}, f32[8,32,2,8,128]{4,1,3,2,0:T(8,128)}, u32[]{:S(2)}) copy-start(f32[8,32,2,8,128]{4,1,3,2,0:T(8,128)} %get-tuple-element.465) | copy-start | bytes 6291460
  107.6 3.3 %copy-start.3 = (f32[8,2,8,32,32]{3,4,2,1,0:T(8,128)S(1)}, f32[8,2,8,32,32]{3,4,2,1,0:T(8,128)}, u32[]{:S(2)}) copy-start(f32[8,2,8,32,32]{3,4,2,1,0:T(8,128)} %copy-done.2) | copy-start | bytes 1572868
  107.6 3.3 %copy-start.22 = (bf16[2,128,2,128]{3,1,0,2:T(8,128)(2,1)S(1)}, bf16[2,128,2,128]{3,1,0,2:T(8,128)(2,1)}, u32[]{:S(2)}) copy-start(bf16[2,128,2,128]{3,1,0,2:T(8,128)(2,1)} %copy-done.21) | copy-start | bytes 393220
  107.6 6.1 %copy-start.12 = (f32[8,2,32,32,8]{3,2,4,1,0:T(8,128)S(1)}, f32[8,2,32,32,8]{3,2,4,1,0:T(8,128)}, u32[]{:S(2)}) copy-start(f32[8,2,32,32,8]{3,2,4,1,0:T(8,128)} %fusion.52) | copy-start | bytes 1572868
  110.9 2.8 %copy-start.9 = (f32[8,2,32,32,8]{3,2,4,1,0:T(8,128)S(1)}, f32[8,2,32,32,8]{3,2,4,1,0:T(8,128)}, u32[]{:S(2)}) copy-start(f32[8,2,32,32,8]{3,2,4,1,0:T(8,128)} %copy-done.8) | copy-start | bytes 1572868
  110.9 2.8 %copy-start.11 = (bf16[2,128,16,128]{3,2,1,0:T(8,128)(2,1)S(1)}, bf16[2,128,16,128]{3,2,1,0:T(8,128)(2,1)}, u32[]{:S(2)}) copy-start(bf16[2,128,16,128]{3,2,1,0:T(8,128)(2,1)} %copy-done.10) | copy-start | bytes 3145732
  114.7 2.9 %copy-start.25 = (f32[1,8,32,2,128]{4,2,3,1,0:T(8,128)S(1)}, f32[1,8,32,2,128]{4,2,3,1,0:T(8,128)}, u32[]{:S(2)}) copy-start(f32[1,8,32,2,128]{4,2,3,1,0:T(8,128)} %convolution_bitcast_fusion.4) | copy-start | bytes 786436
  117.7 2.4 %copy-start.13 = (bf16[8,2,8,32,32]{3,4,2,1,0:T(8,128)(2,1)S(1)}, bf16[8,2,8,32,32]{3,4,2,1,0:T(8,128)(2,1)}, u32[]{:S(2)}) copy-start(bf16[8,2,8,32,32]{3,4,2,1,0:T(8,128)(2,1)} %fusion.28) | copy-start | bytes 786436
  117.7 2.4 %copy-start.20 = (bf16[2,128,2,128]{3,1,0,2:T(8,128)(2,1)S(1)}, bf16[2,128,2,128]{3,1,0,2:T(8,128)(2,1)}, u32[]{:S(2)}) copy-start(bf16[2,128,2,128]{3,1,0,2:T(8,128)(2,1)} %copy-done.19) | copy-start | bytes 393220
  123.0 4.1 %copy-start.5 = (f32[2,32,2,128,16]{3,2,1,4,0:T(2,128)S(1)}, f32[2,32,2,128,16]{3,2,1,4,0:T(2,128)}, u32[]{:S(2)}) copy-start(f32[2,32,2,128,16]{3,2,1,4,0:T(2,128)} %get-tuple-element.863) | copy-start | bytes 3145732 | tf_op jit(solution)/shard_map/while
  132.4 17.6 %all-to-all-start.6 = ((bf16[256,16,128]{2,1,0:T(8,128)(2,1)}), bf16[256,16,128]{2,1,0:T(8,128)(2,1)S(1)}, u32[]{:S(2)}, u32[]{:S(2)}) async-start(bf16[256,16,128]{2,1,0:T(8,128)(2,1)} %bitcast.69), calls=%async_computation.6 | async-start | bytes 2097152 | tf_op jit(solution)/shard_map/all_to_all | solution.py:168
  136.1 48.0 %copy-start.26 = (pred[16]{0:T(512)(128)(4,1)S(1)}, pred[16]{0:T(512)(128)(4,1)}, u32[]{:S(2)}) copy-start(pred[16]{0:T(512)(128)(4,1)} %get-tuple-element.620) | copy-start | bytes 52
  136.1 48.0 %copy-start.28 = (s32[16]{0:T(128)S(1)}, s32[16]{0:T(128)}, u32[]{:S(2)}) copy-start(s32[16]{0:T(128)} %copy-done.27) | copy-start | bytes 196
  150.0 29.1 %copy-start.14 = (bf16[256,16,128]{2,1,0:T(8,128)(2,1)}, bf16[256,16,128]{2,1,0:T(8,128)(2,1)S(1)}, u32[]{:S(2)}) copy-start(bf16[256,16,128]{2,1,0:T(8,128)(2,1)S(1)} %all-to-all-done.6) | copy-start | bytes 3145732
  179.1 7.4 %copy-start.4 = (f32[8,2,8,32,32]{3,4,2,1,0:T(8,128)S(1)}, f32[8,2,8,32,32]{3,4,2,1,0:T(8,128)}, u32[]{:S(2)}) copy-start(f32[8,2,8,32,32]{3,4,2,1,0:T(8,128)} %copy-done.2) | copy-start | bytes 1572868
  179.1 7.4 %copy-start.7 = (bf16[2,128,16,128]{3,2,1,0:T(8,128)(2,1)S(1)}, bf16[2,128,16,128]{3,2,1,0:T(8,128)(2,1)}, u32[]{:S(2)}) copy-start(bf16[2,128,16,128]{3,2,1,0:T(8,128)(2,1)} %copy-done.6) | copy-start | bytes 3145732
  179.1 19.6 %all-to-all-start.4 = ((bf16[256,16,128]{2,1,0:T(8,128)(2,1)}), bf16[256,16,128]{2,1,0:T(8,128)(2,1)}, u32[]{:S(2)}, u32[]{:S(2)}) async-start(bf16[256,16,128]{2,1,0:T(8,128)(2,1)} %bitcast.252), calls=%async_computation.4 | async-start | bytes 2097152 | tf_op jit(solution)/shard_map/all_to_all | solution.py:167
  186.5 0.8 copy-start.23
  187.3 22.6 %copy-start.15 = (bf16[256,16,128]{2,1,0:T(8,128)(2,1)S(1)}, bf16[256,16,128]{2,1,0:T(8,128)(2,1)}, u32[]{:S(2)}) copy-start(bf16[256,16,128]{2,1,0:T(8,128)(2,1)} %copy-done.14) | copy-start | bytes 3145732
  198.7 7.8 %all-to-all-start.9 = ((bf16[256,2,128]{2,1,0:T(2,128)(2,1)}), bf16[256,2,128]{2,1,0:T(2,128)(2,1)S(1)}, u32[]{:S(2)}, u32[]{:S(2)}) async-start(bf16[256,2,128]{2,1,0:T(2,128)(2,1)} %copy.136), calls=%async_computation.9 | async-start | bytes 262144 | tf_op jit(solution)/shard_map/all_to_all | solution.py:172
  206.6 7.8 %all-to-all-start.8 = ((bf16[256,2,128]{2,1,0:T(2,128)(2,1)}), bf16[256,2,128]{2,1,0:T(2,128)(2,1)S(1)}, u32[]{:S(2)}, u32[]{:S(2)}) async-start(bf16[256,2,128]{2,1,0:T(2,128)(2,1)} %copy.131), calls=%async_computation.8 | async-start | bytes 262144 | tf_op jit(solution)/shard_map/all_to_all | solution.py:171
where the time goes:
time: 217 us; the launch traced here: 215 us
  waiting for transfers between devices  60.3 us (28%)
  starting transfers between devices  35.9 us (17%)
  local copies, waits for them, and re-layouts  35.3 us (16%)
  matrix products  32.2 us (15%)
  blocking collectives  29.1 us (13%)
  other arithmetic  17.1 us (8%)
  loops' own time  4.02 us (2%)
    all_to_all x1, blocking collectives, on_device(): lax.all_to_all(far_grads, 'grp', split_axis=1, concat_axis=1, tiled=True)  29.1 us
    all_to_all x1, waiting for transfers between devices, on_device(): lax.all_to_all(query_rows, 'uly', split_axis=0, concat_axis=1, tiled=True)  13.9 us
    all_to_all x1, waiting for transfers between devices, on_device(): lax.all_to_all(queries, 'uly', split_axis=1, concat_axis=0, tiled=True)  12.9 us
    unnamed x57, local copies, waits for them, and re-layouts  12.2 us
    all_to_all x1, waiting for transfers between devices, on_device(): lax.all_to_all(attended_rows, 'uly', split_axis=0, concat_axis=1, tiled=T...  10.6 us
    all_to_all x1, waiting for transfers between devices, on_device(): lax.all_to_all(output_cotangent, 'uly', split_axis=1, concat_axis=0, tile...  9.72 us
    all_to_all x1, waiting for transfers between devices, on_device(): lax.all_to_all(outgoing, 'grp', split_axis=1, concat_axis=1, tiled=True)  7.02 us
    dot_general x2, matrix products, backward(): jnp.einsum('pkgqj,pjkd->pqkgd', dscores, key_rows, preferred_element_type...  5.96 us
  transfers between devices with their start and end apart: 9, of which 8 were waited for; matrix products, arithmetic and copies ran while one was open for 13% of the time, Pallas kernels for 0%

commit v1 on v0

--- a/solution.py
+++ b/solution.py
@@ -2,6 +2,17 @@
 import jax.numpy as jnp
 from jax import lax
 from jax.sharding import PartitionSpec as P
+
+
+def in_blocks(x, dim, size):
+    before, after = (x.shape[:dim], x.shape[dim + 1 :])
+    return jnp.moveaxis(x.reshape(*before, size, -1, *after), dim, 0)
+
+
+def joined_along(blocks, dim):
+    shape = list(blocks.shape[1:])
+    shape[dim] *= blocks.shape[0]
+    return jnp.moveaxis(blocks, 0, dim).reshape(shape)
 
 
 def on_device(queries, keys, values, output_cotangent, block_lists, list_counts):
@@ -40,7 +51,14 @@
     )
     stacked = jnp.stack([to_blocks(key_heads), to_blocks(value_heads)])
     outgoing = jnp.take(stacked, send_place, axis=1)
-    arrived = lax.all_to_all(outgoing, "grp", split_axis=1, concat_axis=1, tiled=True)
+    size, index = (lax.axis_size("grp"), lax.axis_index("grp"))
+    tiles = in_blocks(outgoing, 1, size)
+    outs = [tiles[index]]
+    for lap in range(1, size):
+        sent = tiles[index ^ lap]
+        outs.append(lax.ppermute(sent, "grp", [(i, i ^ lap) for i in range(size)]))
+    tiles = jnp.stack(outs)[index ^ jnp.arange(size)]
+    arrived = joined_along(tiles, 1)
     kv_local = key_heads.shape[1]
     heads_local = query_heads.shape[1]
     heads_per_group = heads_local // kv_local

time: 217 us -> 208 us (0.959)
  waiting for transfers between devices: 60.3 us -> 37.4 us
  starting transfers between devices: 35.9 us -> 52.3 us
  other arithmetic: 17.1 us -> 14.4 us
    ppermute x0 -> x15, starting transfers between devices: none -> 21.7 us  [on_device(): outs.append(lax.ppermute(sent, 'grp', [(i, i ^ lap) for i in range(size)]))]
    all_to_all x1, waiting for transfers between devices: 12.9 us -> 0.01 us  [on_device(): lax.all_to_all(queries, 'uly', split_axis=1, concat_axis=0, tiled=True)]
    all_to_all x1, waiting for transfers between devices: 9.72 us -> 0.01 us  [on_device(): lax.all_to_all(output_cotangent, 'uly', split_axis=1, concat_axis=0, tile...]
    all_to_all x1 -> x0, waiting for transfers between devices: 7.02 us -> none  [on_device(): lax.all_to_all(outgoing, 'grp', split_axis=1, concat_axis=1, tiled=True)]
    ppermute x0 -> x15, waiting for transfers between devices: none -> 5.92 us  [on_device(): outs.append(lax.ppermute(sent, 'grp', [(i, i ^ lap) for i in range(size)]))]
    all_to_all x1 -> x0, starting transfers between devices: 5.91 us -> none  [on_device(): lax.all_to_all(outgoing, 'grp', split_axis=1, concat_axis=1, tiled=True)]
    unnamed x57 -> x66, local copies, waits for them, and re-layouts: 12.2 us -> 12.9 us
  transfers between devices with their start and end apart: 9 -> 23, of which waited for: 8 -> 8; matrix products, arithmetic and copies ran while one was open for 13% -> 21% of each run, Pallas kernels for 0% -> 0%
where the time goes in v1:
time: 208 us; the launch traced here: 206 us
  starting transfers between devices  52.3 us (25%)
  waiting for transfers between devices  37.4 us (18%)
  local copies, waits for them, and re-layouts  34.9 us (17%)
  matrix products  33.2 us (16%)
  blocking collectives  28.3 us (14%)
  other arithmetic  14.4 us (7%)
  loops' own time  4.34 us (2%)
    all_to_all x1, blocking collectives, on_device(): lax.all_to_all(far_grads, 'grp', split_axis=1, concat_axis=1, tiled=True)  28.3 us
    ppermute x15, starting transfers between devices, on_device(): outs.append(lax.ppermute(sent, 'grp', [(i, i ^ lap) for i in range(size)]))  21.7 us
    all_to_all x1, waiting for transfers between devices, on_device(): lax.all_to_all(query_rows, 'uly', split_axis=0, concat_axis=1, tiled=True)  14.4 us
    unnamed x66, local copies, waits for them, and re-layouts  12.9 us
    all_to_all x1, waiting for transfers between devices, on_device(): lax.all_to_all(attended_rows, 'uly', split_axis=0, concat_axis=1, tiled=T...  10.9 us
    dot_general x2, matrix products, backward(): jnp.einsum('pkgqj,pjkd->pqkgd', dscores, key_rows, preferred_element_type...  6.01 us
    dot_general x2, matrix products, backward(): jnp.einsum('pqkgd,pjkd->pkgqj', grad_blk, value_rows, preferred_element_t...  5.95 us
    ppermute x15, waiting for transfers between devices, on_device(): outs.append(lax.ppermute(sent, 'grp', [(i, i ^ lap) for i in range(size)]))  5.92 us
  transfers between devices with their start and end apart: 23, of which 8 were waited for; matrix products, arithmetic and copies ran while one was open for 21% of the time, Pallas kernels for 0%

profile of v1, /device:TPU:0, one launch (start us, length us, event | category | flops | bytes accessed | tf_op | source)
XLA Modules:
  0.0 206.2 jit_solution(7025686496187461987)
XLA Ops:
  0.6 1.7 copy.90
  2.3 4.2 %all-to-all-start = ((bf16[128,4,128]{2,0,1:T(8,128)(2,1)}), bf16[128,4,128]{2,0,1:T(8,128)(2,1)S(1)}, u32[]{:S(2)}, u32[]{:S(2)}) async-start(bf16[128,4,128]{2,0,1:T(8,128)(2,1)} %copy.90), calls=%async_computation | async-start | bytes 262144 | tf_op jit(solution)/shard_map/all_to_all | solution.py:49
  7.1 1.3 reduce.3
  8.5 0.7 broadcast_compare_fusion
  9.6 1.6 copy.98
  11.2 2.6 %copy.92 = bf16[128,32,128]{2,0,1:T(8,128)(2,1)} copy(bf16[128,32,128]{2,1,0:T(8,128)(2,1)} %param.14) | data formatting | bytes 2097152 | tf_op args[0]
  13.8 1.4 copy.110
  15.2 0.7 convert_reduce_fusion
  15.9 3.4 %all-to-all-start.2 = ((bf16[128,4,128]{2,0,1:T(8,128)(2,1)}), bf16[128,4,128]{2,0,1:T(8,128)(2,1)S(1)}, u32[]{:S(2)}, u32[]{:S(2)}) async-start(bf16[128,4,128]{2,0,1:T(8,128)(2,1)} %copy.98), calls=%async_computation.2 | async-start | bytes 262144 | tf_op jit(solution)/shard_map/all_to_all | solution.py:50
  19.3 4.5 %all-to-all-done.2 = bf16[128,4,128]{2,0,1:T(8,128)(2,1)S(1)} async-done(((bf16[128,4,128]{2,0,1:T(8,128)(2,1)}), bf16[128,4,128]{2,0,1:T(8,128)(2,1)S(1)}, u32[]{:S(2)}, u32[]{:S(2)}) %all-to-all-start.2) | async-done | bytes 131104 | tf_op jit(solution)/shard_map/all_to_all | solution.py:50
  23.8 3.6 %all-to-all-start.1 = ((bf16[128,32,128]{2,0,1:T(8,128)(2,1)}), bf16[128,32,128]{2,0,1:T(8,128)(2,1)S(1)}, u32[]{:S(2)}, u32[]{:S(2)}) async-start(bf16[128,32,128]{2,0,1:T(8,128)(2,1)} %copy.92), calls=%async_computation.1 | async-start | bytes 2097152 | tf_op jit(solution)/shard_map/all_to_all | solution.py:47
  29.2 2.1 collective-permute-start.1
  31.3 1.8 collective-permute-start.3
  33.1 2.6 %collective-permute-start.5 = (bf16[2,1,32,2,128]{4,2,3,0,1:T(8,128)(2,1)S(1)}, bf16[2,1,32,2,128]{4,2,3,0,1:T(8,128)(2,1)S(1)}, u32[]{:S(2)}, u32[]{:S(2)}) collective-permute-start(bf16[2,1,32,2,128]{4,2,3,0,1:T(8,128)(2,1)S(1)} %get-tuple-element.639), channel_id=1, source_target_pairs={{0,12},{2,14},{4,8},{6,10},{8,4},{10,6},{12,0},{14,2},{16,28},{18,... | collective-permute-start | bytes 98312 | tf_op jit(solution)/shard_map/ppermute | solution.py:59
  35.9 2.8 %collective-permute-start.7 = (bf16[2,1,32,2,128]{4,2,3,0,1:T(8,128)(2,1)S(1)}, bf16[2,1,32,2,128]{4,2,3,0,1:T(8,128)(2,1)S(1)}, u32[]{:S(2)}, u32[]{:S(2)}) collective-permute-start(bf16[2,1,32,2,128]{4,2,3,0,1:T(8,128)(2,1)S(1)} %get-tuple-element.637), channel_id=1, source_target_pairs={{0,16},{2,18},{4,20},{6,22},{8,24},{10,26},{12,28},{14,30},{16,0},... | collective-permute-start | bytes 98312 | tf_op jit(solution)/shard_map/ppermute | solution.py:59
  39.0 3.3 %collective-permute-start.9 = (bf16[2,1,32,2,128]{4,2,3,0,1:T(8,128)(2,1)S(1)}, bf16[2,1,32,2,128]{4,2,3,0,1:T(8,128)(2,1)S(1)}, u32[]{:S(2)}, u32[]{:S(2)}) collective-permute-start(bf16[2,1,32,2,128]{4,2,3,0,1:T(8,128)(2,1)S(1)} %get-tuple-element.635), channel_id=1, source_target_pairs={{0,20},{2,22},{4,16},{6,18},{8,28},{10,30},{12,24},{14,26},{16,4},... | collective-permute-start | bytes 98312 | tf_op jit(solution)/shard_map/ppermute | solution.py:59
  42.5 3.7 %collective-permute-start.11 = (bf16[2,1,32,2,128]{4,2,3,0,1:T(8,128)(2,1)S(1)}, bf16[2,1,32,2,128]{4,2,3,0,1:T(8,128)(2,1)S(1)}, u32[]{:S(2)}, u32[]{:S(2)}) collective-permute-start(bf16[2,1,32,2,128]{4,2,3,0,1:T(8,128)(2,1)S(1)} %get-tuple-element.633), channel_id=1, source_target_pairs={{0,24},{2,26},{4,28},{6,30},{8,16},{10,18},{12,20},{14,22},{16,8},... | collective-permute-start | bytes 98312 | tf_op jit(solution)/shard_map/ppermute | solution.py:59
  46.4 4.3 %collective-permute-start.13 = (bf16[2,1,32,2,128]{4,2,3,0,1:T(8,128)(2,1)S(1)}, bf16[2,1,32,2,128]{4,2,3,0,1:T(8,128)(2,1)S(1)}, u32[]{:S(2)}, u32[]{:S(2)}) collective-permute-start(bf16[2,1,32,2,128]{4,2,3,0,1:T(8,128)(2,1)S(1)} %get-tuple-element.631), channel_id=1, source_target_pairs={{0,28},{2,30},{4,24},{6,26},{8,20},{10,22},{12,16},{14,18},{16,12}... | collective-permute-start | bytes 98312 | tf_op jit(solution)/shard_map/ppermute | solution.py:59
  51.6 1.9 collective-permute-done.13
  53.5 3.4 %collective-permute-done.14 = bf16[2,1,32,2,128]{4,2,3,0,1:T(8,128)(2,1)S(1)} collective-permute-done((bf16[2,1,32,2,128]{4,2,3,0,1:T(8,128)(2,1)S(1)}, bf16[2,1,32,2,128]{4,2,3,0,1:T(8,128)(2,1)S(1)}, u32[]{:S(2)}, u32[]{:S(2)}) %collective-permute-start.14) | collective-permute-done | bytes 32800 | tf_op jit(solution)/shard_map/ppermute | solution.py:59
  58.9 4.4 %all-to-all-start.4 = ((bf16[128,32,128]{2,0,1:T(8,128)(2,1)}), bf16[128,32,128]{2,0,1:T(8,128)(2,1)}, u32[]{:S(2)}, u32[]{:S(2)}) async-start(bf16[128,32,128]{2,0,1:T(8,128)(2,1)} %copy.110), calls=%async_computation.4 | async-start | bytes 2097152 | tf_op jit(solution)/shard_map/all_to_all | solution.py:48
  63.3 0.7 copy.94
  64.0 1.8 fusion.57
  65.8 1.3 copy-done.8
  67.1 3.0 %copy.103 = f32[8,2,32,32,8]{3,4,2,1,0:T(8,128)} copy(f32[8,2,32,32,8]{3,2,4,1,0:T(8,128)S(1)} %fusion.57) | data formatting | bytes 1048576 | tf_op jit(solution)/shard_map/while | solution.py:106
  70.2 1.9 copy.107
  72.1 2.7 %fusion.98 = (f32[8,2,8,32]{3,2,1,0:T(8,128)S(1)}, f32[8,2,8,32,32]{3,4,2,1,0:T(8,128)S(1)}) fusion(bf16[8,32,2,8,128]{4,3,2,1,0:T(8,128)(2,1)S(1)} %bitcast.315, bf16[8,32,2,128,1]{3,1,0,2,4:T(8,128)(2,1)} %bitcast.322, pred[32,32]{0,1:T(8,128)(4,1)S(1)} %iota_compare_fusion), kind=kOutput, calls=%fused_computation.187 | convolution fusion | flops 33943552 | bytes 1721344 | tf_op jit(solution)/shard_map/pqkgd,pjkd->pkgqj/dot_general | solution.py:75
  74.8 1.3 copy-done.2
  76.1 0.7 exponential_reduce_fusion
  76.8 4.2 %while.43 = (s32[]{:T(128)}, f32[8,2,8,32]{3,2,1,0:T(8,128)S(1)}, f32[8,2,8,32]{3,2,1,0:T(8,128)S(1)}, s32[]{:T(128)}, pred[8,1]{0,1:T(4,128)(4,1)S(1)}, /*index=5*/f32[8,2,32,32,8]{3,4,2,1,0:T(8,128)}, s32[]{:T(128)}) while((s32[]{:T(128)}, f32[8,2,8,32]{3,2,1,0:T(8,128)S(1)}, f32[8,2,8,32]{3,2,1,0:T(8,128)S(1)}, s32[]{:T(128)}, ...), condition=%wide.region_7.9_spmd, body=%wide.region_4.8_spmd.sunk | while | flops 925698 | bytes 3358841 | solution.py:106
  77.5 2.1 %bitcast_reduce_fusion.2 = f32[8,2,8,32]{3,2,1,0:T(8,128)S(1)} fusion(f32[8,2,32,32,8]{3,4,2,1,0:T(8,128)} %get-tuple-element.820, pred[8]{0:T(512)(128)(4,1)S(1)} %bitcast.342), kind=kLoop, calls=%fused_computation.5.clone.1 | loop fusion | flops 389120 | bytes 540680 | tf_op jit(solution)/shard_map/while/body/reduce_max | solution.py:100
  81.1 3.5 %convolution_bitcast_fusion.1 = f32[8,32,2,8,128]{4,1,3,2,0:T(8,128)} fusion(f32[8,2,8,32,32]{3,4,2,1,0:T(8,128)} %copy-done.2, f32[8,2,8,32]{3,2,1,0:T(8,128)S(1)} %log_add_fusion, bf16[8,32,2,128,1]{3,1,0,2,4:T(8,128)(2,1)S(1)} %bitcast.325), kind=kOutput, calls=%fused_computation.53 | convolution fusion | flops 33816576 | bytes 2768896 | tf_op jit(solution)/shard_map/pkgqj,pjkd->pqkgd/dot_general | solution.py:112
  84.6 4.8 %while.44 = (s32[]{:T(128)}, f32[8,32,2,8,128]{4,1,3,2,0:T(8,128)}, s32[]{:T(128)}, pred[8,1]{0,1:T(4,128)(4,1)S(1)}, f32[8,2,32,32,8]{2,3,4,1,0:T(8,128)S(1)}, ...) while((s32[]{:T(128)}, f32[8,32,2,8,128]{4,1,3,2,0:T(8,128)}, s32[]{:T(128)}, ...), condition=%wide.region_9.11_spmd, body=%wide.region_8.10_spmd.sunk | while | flops 34603008 | bytes 4866141 | solution.py:126
  85.3 3.3 %bitcast_add_fusion.6 = f32[8,32,2,8,128]{4,1,3,2,0:T(8,128)} fusion(f32[8,32,2,8,128]{4,1,3,2,0:T(8,128)} %get-tuple-element.831, f32[8,2,32,32,8]{2,3,4,1,0:T(8,128)S(1)} %get-tuple-element.842, f32[8,2,8,32]{3,2,1,0:T(8,128)S(1)} %get-tuple-element.843, pred[8]{0:T(512)(128)(4,1)S(1)} %bitcast.344, bf16[8,32,2,128]{3,1,2,0:T(8,128)(2,1)S(1)} %get-tuple-element.844), kind=kOutput, calls=%fused_computation.10.clone.1 | convolution fusion | flops 34603008 | bytes 4866056 | tf_op jit(solution)/shard_map/while/body/pkgqj,pjkd->pqkgd/dot_general | solution.py:122
  89.5 1.9 copy.112
  91.4 3.2 %fusion.52 = f32[8,2,32,32,8]{3,2,4,1,0:T(8,128)} fusion(bf16[8,32,2,8,128]{4,3,2,1,0:T(8,128)(2,1)S(1)} %bitcast.309, bf16[8,32,2,128]{3,1,2,0:T(8,128)(2,1)S(1)} %get-tuple-element.885), kind=kOutput, calls=%fused_computation.77 | convolution fusion | flops 33554432 | bytes 1703936 | tf_op jit(solution)/shard_map/while/body/pqkgd,pjkd->pkgqj/dot_general | solution.py:136
  94.6 3.2 %multiply_reduce_fusion = (f32[8,32,2,8]{3,2,1,0:T(2,128)}, bf16[8,32,2,8,128]{4,3,2,1,0:T(8,128)(2,1)}) fusion(bf16[8,32,2,8,128]{4,3,2,1,0:T(8,128)(2,1)S(1)} %bitcast.310, f32[8,32,2,8,128]{4,1,3,2,0:T(8,128)S(1)} %copy-done.1), kind=kLoop, calls=%fused_computation.48 | loop fusion | flops 2093056 | bytes 4210688 | tf_op jit(solution)/shard_map/reduce_sum | solution.py:129
  97.8 1.0 copy.115
  98.8 3.3 %convolution_bitcast_fusion.4 = f32[1,8,32,2,128]{4,2,3,1,0:T(8,128)} fusion(f32[8,2,32,32,8]{3,2,4,1,0:T(8,128)} %copy-done.8, f32[8,2,8,32]{3,2,1,0:T(8,128)S(1)} %get-tuple-element.883, pred[8]{0:T(512)(128)(4,1)S(1)} %get-tuple-element.627, bf16[8,32,2,8,128]{4,3,2,1,0:T(8,128)(2,1)S(1)} %bitcast.311), kind=kOutput, calls=%fused_computation.57 | convolution fusion | flops 34078720 | bytes 1851400 | tf_op jit(solution)/shard_map/while/body/pkgqj,pqkgd->pjkd/dot_general | solution.py:147
  102.1 2.8 %fusion.28 = bf16[8,2,8,32,32]{3,4,2,1,0:T(8,128)(2,1)} fusion(f32[8,2,8,32,32]{3,4,2,1,0:T(8,128)S(1)} %copy-done.3, f32[8,2,8,32]{3,2,1,0:T(8,128)S(1)} %copy.115, f32[8,2,8,32]{3,2,1,0:T(8,128)S(1)} %get-tuple-element.883, bf16[8,32,2,8,128]{4,3,2,1,0:T(8,128)(2,1)S(1)} %bitcast.312, bf16[8,32,2,128,1]{3,1,0,2,4:T(8,128)(2,1)S(1)} %bitcast.326), kind=kOutput, calls=%fused_computation.43 | convolution fusion | flops 34078720 | bytes 1998848 | tf_op jit(solution)/shard_map/pqkgd,pjkd->pkgqj/dot_general | solution.py:136
  104.9 1.0 fusion.33
  105.9 3.0 %copy.123 = f32[8,2,32,32,8]{2,3,4,1,0:T(8,128)} copy(f32[8,2,32,32,8]{3,2,4,1,0:T(8,128)} %fusion.52) | data formatting | bytes 1048576 | tf_op jit(solution)/shard_map/while | solution.py:172
  108.9 0.9 fusion.60
  109.8 1.5 copy.125
  111.3 1.9 convolution_bitcast_fusion
  113.7 6.1 %while.45 = (s32[]{:T(128)}, f32[8,32,2,8,128]{4,1,3,2,0:T(8,128)}, f32[2,16,32,2,128]{4,3,2,1,0:T(2,128)S(1)}, s32[]{:T(128)}, pred[8,1]{0,1:T(4,128)(4,1)S(1)}...) while((s32[]{:T(128)}, f32[8,32,2,8,128]{4,1,3,2,0:T(8,128)}, ...), condition=%wide.region_12.14_spmd, body=%wide.region_11.13_spmd.sunk | while | flops 35127296 | bytes 12746905 | solution.py:172
  114.4 4.1 %bitcast_add_fusion.7 = f32[8,32,2,8,128]{4,1,3,2,0:T(8,128)} fusion(f32[8,32,2,8,128]{4,1,3,2,0:T(8,128)} %get-tuple-element.859, f32[8,2,32,32,8]{2,3,4,1,0:T(8,128)} %get-tuple-element.877, f32[8,2,32,32,8]{2,3,4,1,0:T(8,128)S(1)} %get-tuple-element.875, f32[8,2,8,32]{3,2,1,0:T(8,128)S(1)} %get-tuple-element.878, ...), kind=kOutput, calls=%fused_computation.21.clone.1 | convolution fusion | flops 34865152 | bytes 5406728 | tf_op jit(solution)/shard_map/while/body/pkgqj,pjkd->pqkgd/dot_general | solution.py:140
  119.8 3.9 %fusion.29 = bf16[8,32,2,8,128]{4,3,2,1,0:T(8,128)(2,1)} fusion(f32[8,32,2,8,128]{4,1,3,2,0:T(8,128)} %get-tuple-element.466), kind=kLoop, calls=%fused_computation.46 | loop fusion | flops 1048576 | bytes 3145728 | tf_op jit(solution)/shard_map/convert_element_type | solution.py:182
  123.8 3.6 %all-to-all-start.5 = ((bf16[256,16,128]{2,1,0:T(8,128)(2,1)}), bf16[256,16,128]{2,1,0:T(8,128)(2,1)S(1)}, u32[]{:S(2)}, u32[]{:S(2)}) async-start(bf16[256,16,128]{2,1,0:T(8,128)(2,1)} %bitcast.106), calls=%async_computation.5 | async-start | bytes 2097152 | tf_op jit(solution)/shard_map/all_to_all | solution.py:186
  127.5 14.4 %all-to-all-done.5 = bf16[256,16,128]{2,1,0:T(8,128)(2,1)S(1)} async-done(((bf16[256,16,128]{2,1,0:T(8,128)(2,1)}), bf16[256,16,128]{2,1,0:T(8,128)(2,1)S(1)}, u32[]{:S(2)}, u32[]{:S(2)}) %all-to-all-start.5) | async-done | bytes 1048608 | tf_op jit(solution)/shard_map/all_to_all | solution.py:186
  141.8 28.3 %all_to_all.119 = f32[2,16,32,2,128]{4,3,2,0,1:T(2,128)} all-to-all(f32[2,16,32,2,128]{4,3,2,0,1:T(2,128)S(1)} %copy.129), channel_id=1, replica_groups=mesh['grp'=16,'uly'=2] {'grp'}, dimensions={1} | all-to-all | bytes 2097152 | tf_op jit(solution)/shard_map/all_to_all | solution.py:176
  170.1 4.7 %all-to-all-start.3 = ((bf16[256,16,128]{2,1,0:T(8,128)(2,1)}), bf16[256,16,128]{2,1,0:T(8,128)(2,1)}, u32[]{:S(2)}, u32[]{:S(2)}) async-start(bf16[256,16,128]{2,1,0:T(8,128)(2,1)} %bitcast.318), calls=%async_computation.3 | async-start | bytes 2097152 | tf_op jit(solution)/shard_map/all_to_all | solution.py:185
  174.8 2.2 %fusion.39 = f32[2,32,2,128,8]{3,4,2,1,0:T(8,128)S(1)} fusion(f32[2,16,32,2,128]{4,3,2,0,1:T(2,128)} %all_to_all.119, s32[16]{0:T(128)S(1)} %fusion.72, pred[16]{0:T(512)(128)(4,1)S(1)} %get-tuple-element.620), kind=kOutput, calls=%fused_computation.65 | convolution fusion | flops 25166080 | bytes 1572944 | tf_op jit(solution)/shard_map/sp,xsjkd->xpjkd/dot_general | solution.py:177
  178.1 0.8 copy.138
  178.9 10.9 %all-to-all-done.3 = bf16[256,16,128]{2,1,0:T(8,128)(2,1)} async-done(((bf16[256,16,128]{2,1,0:T(8,128)(2,1)}), bf16[256,16,128]{2,1,0:T(8,128)(2,1)}, u32[]{:S(2)}, u32[]{:S(2)}) %all-to-all-start.3) | async-done | bytes 1048608 | tf_op jit(solution)/shard_map/all_to_all | solution.py:185
  189.7 3.4 %all-to-all-start.8 = ((bf16[256,2,128]{2,1,0:T(2,128)(2,1)}), bf16[256,2,128]{2,1,0:T(2,128)(2,1)S(1)}, u32[]{:S(2)}, u32[]{:S(2)}) async-start(bf16[256,2,128]{2,1,0:T(2,128)(2,1)} %copy.138), calls=%async_computation.8 | async-start | bytes 262144 | tf_op jit(solution)/shard_map/all_to_all | solution.py:190
  193.1 2.1 %fusion.36 = bf16[8,32,2,128]{3,1,2,0:T(8,128)(2,1)S(1)} fusion(bf16[8,2,8,32,32]{3,4,2,1,0:T(8,128)(2,1)} %fusion.28, bf16[8,32,2,8,128]{4,3,2,1,0:T(8,128)(2,1)} %bitcast.316, f32[2,8,32,2,128]{4,2,3,1,0:T(8,128)} %bitcast.329), kind=kOutput, calls=%fused_computation.63 | convolution fusion | flops 33751040 | bytes 1703936 | tf_op jit(solution)/shard_map/pkgqj,pqkgd->pjkd/dot_general | solution.py:144
  195.2 0.8 copy.133
  196.0 1.6 all-to-all-done.8
  197.6 3.4 %all-to-all-start.7 = ((bf16[256,2,128]{2,1,0:T(2,128)(2,1)}), bf16[256,2,128]{2,1,0:T(2,128)(2,1)S(1)}, u32[]{:S(2)}, u32[]{:S(2)}) async-start(bf16[256,2,128]{2,1,0:T(2,128)(2,1)} %copy.133), calls=%async_computation.7 | async-start | bytes 262144 | tf_op jit(solution)/shard_map/all_to_all | solution.py:189
  201.0 1.2 copy.127
  202.1 2.4 %copy.109 = bf16[128,2,16,128]{3,2,1,0:T(8,128)(2,1)} copy(bf16[128,2,16,128]{3,2,0,1:T(8,128)(2,1)} %bitcast.81) | data formatting | bytes 2097152 | tf_op jit(solution)/shard_map/all_to_all | solution.py:185
  204.5 0.8 copy.142
  205.5 0.8 copy.141
  (130 shorter events, 9.5 us)
Async XLA Ops:
  0.6 13.2 %copy-start.22 = (bf16[128,32,128]{2,1,0:T(8,128)(2,1)S(1)}, bf16[128,32,128]{2,1,0:T(8,128)(2,1)}, u32[]{:S(2)}) copy-start(bf16[128,32,128]{2,1,0:T(8,128)(2,1)} %param.17) | copy-start | bytes 3145732
  2.3 13.6 %all-to-all-start = ((bf16[128,4,128]{2,0,1:T(8,128)(2,1)}), bf16[128,4,128]{2,0,1:T(8,128)(2,1)S(1)}, u32[]{:S(2)}, u32[]{:S(2)}) async-start(bf16[128,4,128]{2,0,1:T(8,128)(2,1)} %copy.90), calls=%async_computation | async-start | bytes 262144 | tf_op jit(solution)/shard_map/all_to_all | solution.py:49
  15.9 7.9 %all-to-all-start.2 = ((bf16[128,4,128]{2,0,1:T(8,128)(2,1)}), bf16[128,4,128]{2,0,1:T(8,128)(2,1)S(1)}, u32[]{:S(2)}, u32[]{:S(2)}) async-start(bf16[128,4,128]{2,0,1:T(8,128)(2,1)} %copy.98), calls=%async_computation.2 | async-start | bytes 262144 | tf_op jit(solution)/shard_map/all_to_all | solution.py:50
  19.3 8.1 %copy-start.16 = (bf16[2,128,2,128]{3,1,0,2:T(8,128)(2,1)}, bf16[2,128,2,128]{3,1,0,2:T(8,128)(2,1)S(1)}, u32[]{:S(2)}) copy-start(bf16[2,128,2,128]{3,1,0,2:T(8,128)(2,1)S(1)} %copy.91) | copy-start | bytes 393220
  23.8 35.0 %all-to-all-start.1 = ((bf16[128,32,128]{2,0,1:T(8,128)(2,1)}), bf16[128,32,128]{2,0,1:T(8,128)(2,1)S(1)}, u32[]{:S(2)}, u32[]{:S(2)}) async-start(bf16[128,32,128]{2,0,1:T(8,128)(2,1)} %copy.92), calls=%async_computation.1 | async-start | bytes 2097152 | tf_op jit(solution)/shard_map/all_to_all | solution.py:47
  27.4 0.7 copy-start.18
  29.1 4.1 %collective-permute-start = (bf16[2,1,32,2,128]{4,2,3,0,1:T(8,128)(2,1)S(1)}, bf16[2,1,32,2,128]{4,2,3,0,1:T(8,128)(2,1)S(1)}, u32[]{:S(2)}, u32[]{:S(2)}) collective-permute-start(bf16[2,1,32,2,128]{4,2,3,0,1:T(8,128)(2,1)S(1)} %get-tuple-element.644), channel_id=1, source_target_pairs={{0,2},{2,0},{4,6},{6,4},{8,10},{10,8},{12,14},{14,12},{16,18},{18,... | collective-permute-start | bytes 98312 | tf_op jit(solution)/shard_map/ppermute | solution.py:59
  29.2 6.6 %collective-permute-start.1 = (bf16[2,1,32,2,128]{4,2,3,0,1:T(8,128)(2,1)S(1)}, bf16[2,1,32,2,128]{4,2,3,0,1:T(8,128)(2,1)S(1)}, u32[]{:S(2)}, u32[]{:S(2)}) collective-permute-start(bf16[2,1,32,2,128]{4,2,3,0,1:T(8,128)(2,1)S(1)} %get-tuple-element.643), channel_id=1, source_target_pairs={{0,4},{2,6},{4,0},{6,2},{8,12},{10,14},{12,8},{14,10},{16,20},{18,... | collective-permute-start | bytes 98312 | tf_op jit(solution)/shard_map/ppermute | solution.py:59
  31.3 4.7 %collective-permute-start.2 = (bf16[2,1,32,2,128]{4,2,3,0,1:T(8,128)(2,1)S(1)}, bf16[2,1,32,2,128]{4,2,3,0,1:T(8,128)(2,1)S(1)}, u32[]{:S(2)}, u32[]{:S(2)}) collective-permute-start(bf16[2,1,32,2,128]{4,2,3,0,1:T(8,128)(2,1)S(1)} %get-tuple-element.642), channel_id=1, source_target_pairs={{0,6},{2,4},{4,2},{6,0},{8,14},{10,12},{12,10},{14,8},{16,22},{18,... | collective-permute-start | bytes 98312 | tf_op jit(solution)/shard_map/ppermute | solution.py:59
  31.3 7.4 %collective-permute-start.3 = (bf16[2,1,32,2,128]{4,2,3,0,1:T(8,128)(2,1)S(1)}, bf16[2,1,32,2,128]{4,2,3,0,1:T(8,128)(2,1)S(1)}, u32[]{:S(2)}, u32[]{:S(2)}) collective-permute-start(bf16[2,1,32,2,128]{4,2,3,0,1:T(8,128)(2,1)S(1)} %get-tuple-element.641), channel_id=1, source_target_pairs={{0,8},{2,10},{4,12},{6,14},{8,0},{10,2},{12,4},{14,6},{16,24},{18,... | collective-permute-start | bytes 98312 | tf_op jit(solution)/shard_map/ppermute | solution.py:59
  33.1 5.9 %collective-permute-start.4 = (bf16[2,1,32,2,128]{4,2,3,0,1:T(8,128)(2,1)S(1)}, bf16[2,1,32,2,128]{4,2,3,0,1:T(8,128)(2,1)S(1)}, u32[]{:S(2)}, u32[]{:S(2)}) collective-permute-start(bf16[2,1,32,2,128]{4,2,3,0,1:T(8,128)(2,1)S(1)} %get-tuple-element.640), channel_id=1, source_target_pairs={{0,10},{2,8},{4,14},{6,12},{8,2},{10,0},{12,6},{14,4},{16,26},{18,... | collective-permute-start | bytes 98312 | tf_op jit(solution)/shard_map/ppermute | solution.py:59
  33.1 9.2 %collective-permute-start.5 = (bf16[2,1,32,2,128]{4,2,3,0,1:T(8,128)(2,1)S(1)}, bf16[2,1,32,2,128]{4,2,3,0,1:T(8,128)(2,1)S(1)}, u32[]{:S(2)}, u32[]{:S(2)}) collective-permute-start(bf16[2,1,32,2,128]{4,2,3,0,1:T(8,128)(2,1)S(1)} %get-tuple-element.639), channel_id=1, source_target_pairs={{0,12},{2,14},{4,8},{6,10},{8,4},{10,6},{12,0},{14,2},{16,28},{18,... | collective-permute-start | bytes 98312 | tf_op jit(solution)/shard_map/ppermute | solution.py:59
  35.8 6.8 %collective-permute-start.6 = (bf16[2,1,32,2,128]{4,2,3,0,1:T(8,128)(2,1)S(1)}, bf16[2,1,32,2,128]{4,2,3,0,1:T(8,128)(2,1)S(1)}, u32[]{:S(2)}, u32[]{:S(2)}) collective-permute-start(bf16[2,1,32,2,128]{4,2,3,0,1:T(8,128)(2,1)S(1)} %get-tuple-element.638), channel_id=1, source_target_pairs={{0,14},{2,12},{4,10},{6,8},{8,6},{10,4},{12,2},{14,0},{16,30},{18,... | collective-permute-start | bytes 98312 | tf_op jit(solution)/shard_map/ppermute | solution.py:59
  35.9 10.3 %collective-permute-start.7 = (bf16[2,1,32,2,128]{4,2,3,0,1:T(8,128)(2,1)S(1)}, bf16[2,1,32,2,128]{4,2,3,0,1:T(8,128)(2,1)S(1)}, u32[]{:S(2)}, u32[]{:S(2)}) collective-permute-start(bf16[2,1,32,2,128]{4,2,3,0,1:T(8,128)(2,1)S(1)} %get-tuple-element.637), channel_id=1, source_target_pairs={{0,16},{2,18},{4,20},{6,22},{8,24},{10,26},{12,28},{14,30},{16,0},... | collective-permute-start | bytes 98312 | tf_op jit(solution)/shard_map/ppermute | solution.py:59
  38.7 7.7 %collective-permute-start.8 = (bf16[2,1,32,2,128]{4,2,3,0,1:T(8,128)(2,1)S(1)}, bf16[2,1,32,2,128]{4,2,3,0,1:T(8,128)(2,1)S(1)}, u32[]{:S(2)}, u32[]{:S(2)}) collective-permute-start(bf16[2,1,32,2,128]{4,2,3,0,1:T(8,128)(2,1)S(1)} %get-tuple-element.636), channel_id=1, source_target_pairs={{0,18},{2,16},{4,22},{6,20},{8,26},{10,24},{12,30},{14,28},{16,2},... | collective-permute-start | bytes 98312 | tf_op jit(solution)/shard_map/ppermute | solution.py:59
  39.0 11.8 %collective-permute-start.9 = (bf16[2,1,32,2,128]{4,2,3,0,1:T(8,128)(2,1)S(1)}, bf16[2,1,32,2,128]{4,2,3,0,1:T(8,128)(2,1)S(1)}, u32[]{:S(2)}, u32[]{:S(2)}) collective-permute-start(bf16[2,1,32,2,128]{4,2,3,0,1:T(8,128)(2,1)S(1)} %get-tuple-element.635), channel_id=1, source_target_pairs={{0,20},{2,22},{4,16},{6,18},{8,28},{10,30},{12,24},{14,26},{16,4},... | collective-permute-start | bytes 98312 | tf_op jit(solution)/shard_map/ppermute | solution.py:59
  42.4 8.6 %collective-permute-start.10 = (bf16[2,1,32,2,128]{4,2,3,0,1:T(8,128)(2,1)S(1)}, bf16[2,1,32,2,128]{4,2,3,0,1:T(8,128)(2,1)S(1)}, u32[]{:S(2)}, u32[]{:S(2)}) collective-permute-start(bf16[2,1,32,2,128]{4,2,3,0,1:T(8,128)(2,1)S(1)} %get-tuple-element.634), channel_id=1, source_target_pairs={{0,22},{2,20},{4,18},{6,16},{8,30},{10,28},{12,26},{14,24},{16,6},... | collective-permute-start | bytes 98312 | tf_op jit(solution)/shard_map/ppermute | solution.py:59
  42.5 8.4 %collective-permute-start.11 = (bf16[2,1,32,2,128]{4,2,3,0,1:T(8,128)(2,1)S(1)}, bf16[2,1,32,2,128]{4,2,3,0,1:T(8,128)(2,1)S(1)}, u32[]{:S(2)}, u32[]{:S(2)}) collective-permute-start(bf16[2,1,32,2,128]{4,2,3,0,1:T(8,128)(2,1)S(1)} %get-tuple-element.633), channel_id=1, source_target_pairs={{0,24},{2,26},{4,28},{6,30},{8,16},{10,18},{12,20},{14,22},{16,8},... | collective-permute-start | bytes 98312 | tf_op jit(solution)/shard_map/ppermute | solution.py:59
  46.2 5.3 %collective-permute-start.12 = (bf16[2,1,32,2,128]{4,2,3,0,1:T(8,128)(2,1)S(1)}, bf16[2,1,32,2,128]{4,2,3,0,1:T(8,128)(2,1)S(1)}, u32[]{:S(2)}, u32[]{:S(2)}) collective-permute-start(bf16[2,1,32,2,128]{4,2,3,0,1:T(8,128)(2,1)S(1)} %get-tuple-element.632), channel_id=1, source_target_pairs={{0,26},{2,24},{4,30},{6,28},{8,18},{10,16},{12,22},{14,20},{16,10}... | collective-permute-start | bytes 98312 | tf_op jit(solution)/shard_map/ppermute | solution.py:59
  46.4 7.1 %collective-permute-start.13 = (bf16[2,1,32,2,128]{4,2,3,0,1:T(8,128)(2,1)S(1)}, bf16[2,1,32,2,128]{4,2,3,0,1:T(8,128)(2,1)S(1)}, u32[]{:S(2)}, u32[]{:S(2)}) collective-permute-start(bf16[2,1,32,2,128]{4,2,3,0,1:T(8,128)(2,1)S(1)} %get-tuple-element.631), channel_id=1, source_target_pairs={{0,28},{2,30},{4,24},{6,26},{8,20},{10,22},{12,16},{14,18},{16,12}... | collective-permute-start | bytes 98312 | tf_op jit(solution)/shard_map/ppermute | solution.py:59
  50.8 6.1 %collective-permute-start.14 = (bf16[2,1,32,2,128]{4,2,3,0,1:T(8,128)(2,1)S(1)}, bf16[2,1,32,2,128]{4,2,3,0,1:T(8,128)(2,1)S(1)}, u32[]{:S(2)}, u32[]{:S(2)}) collective-permute-start(bf16[2,1,32,2,128]{4,2,3,0,1:T(8,128)(2,1)S(1)} %get-tuple-element.630), channel_id=1, source_target_pairs={{0,30},{2,28},{4,26},{6,24},{8,22},{10,20},{12,18},{14,16},{16,14}... | collective-permute-start | bytes 98312 | tf_op jit(solution)/shard_map/ppermute | solution.py:59
  58.9 30.6 %all-to-all-start.4 = ((bf16[128,32,128]{2,0,1:T(8,128)(2,1)}), bf16[128,32,128]{2,0,1:T(8,128)(2,1)}, u32[]{:S(2)}, u32[]{:S(2)}) async-start(bf16[128,32,128]{2,0,1:T(8,128)(2,1)} %copy.110), calls=%async_computation.4 | async-start | bytes 2097152 | tf_op jit(solution)/shard_map/all_to_all | solution.py:48
  64.0 8.1 %copy-start.10 = (bf16[2,128,16,128]{3,2,1,0:T(8,128)(2,1)}, bf16[2,128,16,128]{3,2,1,0:T(8,128)(2,1)S(1)}, u32[]{:S(2)}) copy-start(bf16[2,128,16,128]{3,2,1,0:T(8,128)(2,1)S(1)} %copy.94) | copy-start | bytes 3145732
  65.8 1.4 copy-start.8
  74.8 1.4 copy-start.2
  76.8 4.3 %copy-start.19 = (bf16[2,128,2,128]{3,1,0,2:T(8,128)(2,1)S(1)}, bf16[2,128,2,128]{3,1,0,2:T(8,128)(2,1)}, u32[]{:S(2)}) copy-start(bf16[2,128,2,128]{3,1,0,2:T(8,128)(2,1)} %copy-done.18) | copy-start | bytes 393220
  77.5 2.2 %copy-start = (f32[8,2,32,32,8]{3,4,2,1,0:T(8,128)S(1)}, f32[8,2,32,32,8]{3,4,2,1,0:T(8,128)}, u32[]{:S(2)}) copy-start(f32[8,2,32,32,8]{3,4,2,1,0:T(8,128)} %get-tuple-element.820) | copy-start | bytes 1572868 | tf_op jit(solution)/shard_map/while
  91.4 10.7 %copy-start.6 = (bf16[2,128,16,128]{3,2,1,0:T(8,128)(2,1)}, bf16[2,128,16,128]{3,2,1,0:T(8,128)(2,1)S(1)}, u32[]{:S(2)}) copy-start(bf16[2,128,16,128]{3,2,1,0:T(8,128)(2,1)S(1)} %copy.112) | copy-start | bytes 3145732
  91.4 3.2 %copy-start.1 = (f32[8,32,2,8,128]{4,1,3,2,0:T(8,128)S(1)}, f32[8,32,2,8,128]{4,1,3,2,0:T(8,128)}, u32[]{:S(2)}) copy-start(f32[8,32,2,8,128]{4,1,3,2,0:T(8,128)} %get-tuple-element.465) | copy-start | bytes 6291460
  98.8 3.3 %copy-start.3 = (f32[8,2,8,32,32]{3,4,2,1,0:T(8,128)S(1)}, f32[8,2,8,32,32]{3,4,2,1,0:T(8,128)}, u32[]{:S(2)}) copy-start(f32[8,2,8,32,32]{3,4,2,1,0:T(8,128)} %copy-done.2) | copy-start | bytes 1572868
  98.8 3.3 %copy-start.20 = (bf16[2,128,2,128]{3,1,0,2:T(8,128)(2,1)S(1)}, bf16[2,128,2,128]{3,1,0,2:T(8,128)(2,1)}, u32[]{:S(2)}) copy-start(bf16[2,128,2,128]{3,1,0,2:T(8,128)(2,1)} %copy-done.18) | copy-start | bytes 393220
  98.8 6.1 %copy-start.12 = (f32[8,2,32,32,8]{3,2,4,1,0:T(8,128)S(1)}, f32[8,2,32,32,8]{3,2,4,1,0:T(8,128)}, u32[]{:S(2)}) copy-start(f32[8,2,32,32,8]{3,2,4,1,0:T(8,128)} %fusion.52) | copy-start | bytes 1572868
  102.1 2.8 %copy-start.9 = (f32[8,2,32,32,8]{3,2,4,1,0:T(8,128)S(1)}, f32[8,2,32,32,8]{3,2,4,1,0:T(8,128)}, u32[]{:S(2)}) copy-start(f32[8,2,32,32,8]{3,2,4,1,0:T(8,128)} %copy-done.8) | copy-start | bytes 1572868
  102.1 2.8 %copy-start.11 = (bf16[2,128,16,128]{3,2,1,0:T(8,128)(2,1)S(1)}, bf16[2,128,16,128]{3,2,1,0:T(8,128)(2,1)}, u32[]{:S(2)}) copy-start(bf16[2,128,16,128]{3,2,1,0:T(8,128)(2,1)} %copy-done.10) | copy-start | bytes 3145732
  105.9 3.0 %copy-start.23 = (f32[1,8,32,2,128]{4,2,3,1,0:T(8,128)S(1)}, f32[1,8,32,2,128]{4,2,3,1,0:T(8,128)}, u32[]{:S(2)}) copy-start(f32[1,8,32,2,128]{4,2,3,1,0:T(8,128)} %convolution_bitcast_fusion.4) | copy-start | bytes 786436
  108.9 2.4 %copy-start.13 = (bf16[8,2,8,32,32]{3,4,2,1,0:T(8,128)(2,1)S(1)}, bf16[8,2,8,32,32]{3,4,2,1,0:T(8,128)(2,1)}, u32[]{:S(2)}) copy-start(bf16[8,2,8,32,32]{3,4,2,1,0:T(8,128)(2,1)} %fusion.28) | copy-start | bytes 786436
  108.9 2.4 %copy-start.17 = (bf16[2,128,2,128]{3,1,0,2:T(8,128)(2,1)S(1)}, bf16[2,128,2,128]{3,1,0,2:T(8,128)(2,1)}, u32[]{:S(2)}) copy-start(bf16[2,128,2,128]{3,1,0,2:T(8,128)(2,1)} %copy-done.16) | copy-start | bytes 393220
  114.4 4.1 %copy-start.5 = (f32[2,32,2,128,16]{3,2,1,4,0:T(2,128)S(1)}, f32[2,32,2,128,16]{3,2,1,4,0:T(2,128)}, u32[]{:S(2)}) copy-start(f32[2,32,2,128,16]{3,2,1,4,0:T(2,128)} %get-tuple-element.880) | copy-start | bytes 3145732 | tf_op jit(solution)/shard_map/while
  123.8 18.1 %all-to-all-start.5 = ((bf16[256,16,128]{2,1,0:T(8,128)(2,1)}), bf16[256,16,128]{2,1,0:T(8,128)(2,1)S(1)}, u32[]{:S(2)}, u32[]{:S(2)}) async-start(bf16[256,16,128]{2,1,0:T(8,128)(2,1)} %bitcast.106), calls=%async_computation.5 | async-start | bytes 2097152 | tf_op jit(solution)/shard_map/all_to_all | solution.py:186
  141.8 28.3 %copy-start.14 = (bf16[256,16,128]{2,1,0:T(8,128)(2,1)}, bf16[256,16,128]{2,1,0:T(8,128)(2,1)S(1)}, u32[]{:S(2)}) copy-start(bf16[256,16,128]{2,1,0:T(8,128)(2,1)S(1)} %all-to-all-done.5) | copy-start | bytes 3145732
  170.1 7.1 %copy-start.4 = (f32[8,2,8,32,32]{3,4,2,1,0:T(8,128)S(1)}, f32[8,2,8,32,32]{3,4,2,1,0:T(8,128)}, u32[]{:S(2)}) copy-start(f32[8,2,8,32,32]{3,4,2,1,0:T(8,128)} %copy-done.2) | copy-start | bytes 1572868
  170.1 7.1 %copy-start.7 = (bf16[2,128,16,128]{3,2,1,0:T(8,128)(2,1)S(1)}, bf16[2,128,16,128]{3,2,1,0:T(8,128)(2,1)}, u32[]{:S(2)}) copy-start(bf16[2,128,16,128]{3,2,1,0:T(8,128)(2,1)} %copy-done.6) | copy-start | bytes 3145732
  170.1 19.6 %all-to-all-start.3 = ((bf16[256,16,128]{2,1,0:T(8,128)(2,1)}), bf16[256,16,128]{2,1,0:T(8,128)(2,1)}, u32[]{:S(2)}, u32[]{:S(2)}) async-start(bf16[256,16,128]{2,1,0:T(8,128)(2,1)} %bitcast.318), calls=%async_computation.3 | async-start | bytes 2097152 | tf_op jit(solution)/shard_map/all_to_all | solution.py:185
  177.2 0.8 copy-start.21
  178.1 22.9 %copy-start.15 = (bf16[256,16,128]{2,1,0:T(8,128)(2,1)S(1)}, bf16[256,16,128]{2,1,0:T(8,128)(2,1)}, u32[]{:S(2)}) copy-start(bf16[256,16,128]{2,1,0:T(8,128)(2,1)} %copy-done.14) | copy-start | bytes 3145732
  189.7 7.8 %all-to-all-start.8 = ((bf16[256,2,128]{2,1,0:T(2,128)(2,1)}), bf16[256,2,128]{2,1,0:T(2,128)(2,1)S(1)}, u32[]{:S(2)}, u32[]{:S(2)}) async-start(bf16[256,2,128]{2,1,0:T(2,128)(2,1)} %copy.138), calls=%async_computation.8 | async-start | bytes 262144 | tf_op jit(solution)/shard_map/all_to_all | solution.py:190
  197.6 7.8 %all-to-all-start.7 = ((bf16[256,2,128]{2,1,0:T(2,128)(2,1)}), bf16[256,2,128]{2,1,0:T(2,128)(2,1)S(1)}, u32[]{:S(2)}, u32[]{:S(2)}) async-start(bf16[256,2,128]{2,1,0:T(2,128)(2,1)} %copy.133), calls=%async_computation.7 | async-start | bytes 262144 | tf_op jit(solution)/shard_map/all_to_all | solution.py:189
